TPU v7x, 512 devices: a whole 4x4x16 slice. The times are simulated.
512 devices in a mesh: prow: 16 (over z), pcol: 32 (over x, y, core).
Axes of the slice: x: 4, y: 4, z: 16, core: 2. Of those that a mesh axis runs over, the one named last changes fastest.
Arguments:
- matrix: bfloat16 [3, 8192, 1, 16384], P(None, 'prow', None, 'pcol'), may hold values from -6 to 6
- pattern: int32 [48, 32], replicated, may hold values 0 or 1
- inverses: bfloat16 [2, 512, 512], replicated, may hold values from -0.01171875 to 0.01171875
- pivots: int32 [2, 3], replicated, may hold values from 0 to 47, as said below
Outputs:
- factored: bfloat16 [3, 8192, 1, 16384], P(None, 'prow', None, 'pcol')
Inputs may be any that keep to these rules, and one draw needn't show every extreme that they name: pivots[s] = (a, b, c) with a and b block rows in 0 .. 47 and c a block column in 0 .. 31; the 4 numbers a and b over all steps are all different, and so are the 2 numbers c; b mod 16 = (a + 8) mod 16 for every step; block row 0 and block row 47 are among the b, and block column 31 is among the c.
All inputs are finite; a program needn't handle non-finite values.
Results may differ from a plain program's by a relative error of at most 0.0068.
Values may be sent and summed in bfloat16 or wider, within the bound.
A program may use at most 64 MiB of HBM per device.

v0:
```python
import jax
import jax.numpy as jnp
from jax import lax
from jax.sharding import PartitionSpec as P


def partner(value, axis, bit):
    mask = 2**bit
    pairs = [(source, source ^ mask) for source in range(lax.axis_size(axis))]
    return lax.ppermute(value, axis, pairs)


def broadcast(block, axis, source):
    block = jnp.where(lax.axis_index(axis) == source, block, jnp.zeros_like(block))
    return lax.psum(block, axis)


def local(matrix, pattern, inverses, pivots):
    nrow = lax.axis_size("prow")
    ncol = lax.axis_size("pcol")
    my_row = lax.axis_index("prow")
    my_col = lax.axis_index("pcol")
    half_bit = nrow.bit_length() - 2
    row_blocks = matrix.shape[0]
    width = matrix.shape[1]
    col_blocks = matrix.shape[2]
    global_rows = jnp.arange(row_blocks, dtype=jnp.int32) * nrow + my_row
    global_cols = jnp.arange(col_blocks, dtype=jnp.int32) * ncol + my_col
    pick_rows = (
        jnp.arange(pattern.shape[0], dtype=jnp.int32)[None, :] == global_rows[:, None]
    ).astype(jnp.float32)
    pick_cols = (
        jnp.arange(pattern.shape[1], dtype=jnp.int32)[None, :] == global_cols[:, None]
    ).astype(jnp.float32)
    local_pattern = jnp.dot(jnp.dot(pick_rows, pattern.astype(jnp.float32)), pick_cols.T)
    work = matrix * local_pattern.astype(matrix.dtype)[:, None, :, None]
    for step in range(inverses.shape[0]):
        first = pivots[step, 0]
        second = pivots[step, 1]
        column_id = pivots[step, 2]
        owner_first = first % nrow
        slot_first = first // nrow
        owner_second = second % nrow
        slot_second = second // nrow
        row_first = lax.dynamic_index_in_dim(work, slot_first, 0, keepdims=False)
        row_second = lax.dynamic_index_in_dim(work, slot_second, 0, keepdims=False)
        outgoing = jnp.where(my_row == owner_first, row_first, row_second)
        incoming = partner(outgoing, "prow", half_bit)
        work = lax.dynamic_update_index_in_dim(
            work, jnp.where(my_row == owner_first, incoming, row_first), slot_first, 0
        )
        current = lax.dynamic_index_in_dim(work, slot_second, 0, keepdims=False)
        work = lax.dynamic_update_index_in_dim(
            work, jnp.where(my_row == owner_second, incoming, current), slot_second, 0
        )
        pivot_now = lax.dynamic_index_in_dim(work, slot_first, 0, keepdims=False)
        upper = broadcast(pivot_now, "prow", owner_first)
        column = lax.dynamic_index_in_dim(work, column_id // ncol, 2, keepdims=False)
        panel = broadcast(column, "pcol", column_id % ncol)
        multipliers = jnp.dot(
            panel.reshape(row_blocks * width, width),
            inverses[step],
            preferred_element_type=jnp.float32,
        )
        multipliers = multipliers.astype(matrix.dtype)
        product = jnp.dot(
            multipliers,
            upper.reshape(width, col_blocks * width),
            preferred_element_type=jnp.float32,
        )
        product = product.reshape(row_blocks, width, col_blocks, width)
        fresh = (work.astype(jnp.float32) - product).astype(matrix.dtype)
        live_rows = jnp.all(global_rows[:, None] != pivots[None, : step + 1, 0], axis=1)
        live_cols = jnp.all(global_cols[:, None] != pivots[None, : step + 1, 2], axis=1)
        is_column = global_cols == column_id
        left_blocks = multipliers.reshape(row_blocks, width, 1, width)
        mixed = jnp.where(
            live_cols[None, None, :, None],
            fresh,
            jnp.where(is_column[None, None, :, None], left_blocks, work),
        )
        work = jnp.where(live_rows[:, None, None, None], mixed, work)
    return work


def solution(mesh):
    placed = (P(None, "prow", None, "pcol"), P(), P(), P())
    return jax.shard_map(
        local, mesh=mesh, in_specs=placed, out_specs=P(None, "prow", None, "pcol"), check_vma=False
    )
```

profile of v0, /device:TPU:6, one launch (start us, length us, event | category | flops | bytes accessed | tf_op | source)
XLA Modules:
  0.0 692.9 jit_solution(15825533346575529023)
XLA Ops:
  6.5 0.0 all-reduce.5.cloned.1.call-start
  6.5 1.6 fusion.25
  13.5 1.0 fusion.8
  14.5 1.6 broadcast_multiply_fusion
  16.1 0.1 bitcast_select_fusion.4
  16.1 15.7 %collective-permute-start = (bf16[512,1,512]{2,0,1:T(8,128)(2,1)S(1)}, bf16[512,1,512]{2,0,1:T(8,128)(2,1)S(1)}, u32[]{:S(2)}, u32[]{:S(2)}) collective-permute-start(bf16[512,1,512]{2,0,1:T(8,128)(2,1)S(1)} %bitcast_select_fusion.4), channel_id=1, source_target_pairs={{0,256},{32,288},{64,320},{96,352},{128,384},{160,416},{192,448},{... | collective-permute-start | bytes 1572872 | tf_op jit(solution)/shard_map/ppermute | solution.py:10
  33.6 14.7 %collective-permute-done = bf16[512,1,512]{2,0,1:T(8,128)(2,1)S(1)} collective-permute-done((bf16[512,1,512]{2,0,1:T(8,128)(2,1)S(1)}, bf16[512,1,512]{2,0,1:T(8,128)(2,1)S(1)}, u32[]{:S(2)}, u32[]{:S(2)}) %collective-permute-start) | collective-permute-done | bytes 524320 | tf_op jit(solution)/shard_map/ppermute | solution.py:10
  48.3 0.1 bitcast_dynamic-update-slice_fusion.3
  48.5 0.1 bitcast_dynamic-update-slice_fusion.2
  48.7 1.2 broadcast_select_fusion.1
  49.9 0.0 copy-start.1
  49.9 0.0 all-reduce.5.cloned.1.call-update
  49.9 0.0 all-reduce.7.cloned.1.call-start
  50.0 0.8 select_bitcast_fusion.1
  50.8 0.0 all-reduce.7.cloned.1.call-update
  50.9 0.0 all-reduce.9.cloned.1.call-start
  57.6 0.7 broadcast_compare_fusion
  58.3 159.6 %all-reduce.5.cloned.1.call-done = bf16[1536,512]{1,0:T(8,128)(2,1)} async-done(((bf16[1536,512]{1,0:T(8,128)(2,1)}), bf16[1536,512]{1,0:T(8,128)(2,1)}) %all-reduce.5.cloned.1.call-update) | async-done | bytes 1572880 | tf_op jit(solution)/shard_map/psum | solution.py:15
  217.9 0.0 copy-done.1
  217.9 3.5 convolution_convert_fusion.1
  221.4 135.3 %all-reduce.7.cloned.1.call-done = bf16[512,512]{1,0:T(8,128)(2,1)} async-done(((bf16[512,512]{1,0:T(8,128)(2,1)}), bf16[512,512]{1,0:T(8,128)(2,1)}) %all-reduce.7.cloned.1.call-update) | async-done | bytes 524304 | tf_op jit(solution)/shard_map/psum | solution.py:15
  356.7 2.6 select_select_fusion.1
  359.3 0.1 bitcast_select_fusion.1
  359.4 8.3 %collective-permute-start.1 = (bf16[512,1,512]{2,0,1:T(8,128)(2,1)S(1)}, bf16[512,1,512]{2,0,1:T(8,128)(2,1)S(1)}, u32[]{:S(2)}, u32[]{:S(2)}) collective-permute-start(bf16[512,1,512]{2,0,1:T(8,128)(2,1)S(1)} %bitcast_select_fusion.1), channel_id=1, source_target_pairs={{0,256},{32,288},{64,320},{96,352},{128,384},{160,416},{192,448},{... | collective-permute-start | bytes 1572872 | tf_op jit(solution)/shard_map/ppermute | solution.py:10
  369.6 27.0 %collective-permute-done.1 = bf16[512,1,512]{2,0,1:T(8,128)(2,1)S(1)} collective-permute-done((bf16[512,1,512]{2,0,1:T(8,128)(2,1)S(1)}, bf16[512,1,512]{2,0,1:T(8,128)(2,1)S(1)}, u32[]{:S(2)}, u32[]{:S(2)}) %collective-permute-start.1) | collective-permute-done | bytes 524320 | tf_op jit(solution)/shard_map/ppermute | solution.py:10
  396.6 0.1 bitcast_dynamic-update-slice_fusion.1
  396.8 0.1 bitcast_dynamic-update-slice_fusion
  397.0 1.2 broadcast_select_fusion
  398.2 0.0 copy-start
  398.2 0.0 copy-start.2
  398.2 0.0 all-reduce.9.cloned.1.call-update
  398.2 0.0 all-reduce.11.cloned.1.call-start
  399.0 0.0 copy-done
  399.0 0.8 compare_reduce_fusion
  399.8 0.8 select_bitcast_fusion
  400.6 0.0 all-reduce.11.cloned.1.call-update
  400.6 0.1 slice_reduce_fusion
  400.8 0.2 compare_reduce_fusion.1
  400.9 142.3 %all-reduce.9.cloned.1.call-done = bf16[1536,512]{1,0:T(8,128)(2,1)} async-done(((bf16[1536,512]{1,0:T(8,128)(2,1)}), bf16[1536,512]{1,0:T(8,128)(2,1)}) %all-reduce.9.cloned.1.call-update) | async-done | bytes 1572880 | tf_op jit(solution)/shard_map/psum | solution.py:15
  543.2 0.0 copy-done.2
  543.2 3.5 convolution_convert_fusion
  546.8 135.2 %all-reduce.11.cloned.1.call-done = bf16[512,512]{1,0:T(8,128)(2,1)} async-done(((bf16[512,512]{1,0:T(8,128)(2,1)}), bf16[512,512]{1,0:T(8,128)(2,1)}) %all-reduce.11.cloned.1.call-update) | async-done | bytes 524304 | tf_op jit(solution)/shard_map/psum | solution.py:15
  682.0 4.4 select_select_fusion
  (5 shorter events, 0.2 us)
Async XLA Ops:
  6.5 211.3 %all-reduce.5.cloned.1.call-start = ((), (), s32[]{:S(2)}) async-start(), calls=%async_computation | async-start | bytes 3145728 | tf_op jit(solution)/shard_map/psum | solution.py:15
  16.1 32.2 %collective-permute-start = (bf16[512,1,512]{2,0,1:T(8,128)(2,1)S(1)}, bf16[512,1,512]{2,0,1:T(8,128)(2,1)S(1)}, u32[]{:S(2)}, u32[]{:S(2)}) collective-permute-start(bf16[512,1,512]{2,0,1:T(8,128)(2,1)S(1)} %bitcast_select_fusion.4), channel_id=1, source_target_pairs={{0,256},{32,288},{64,320},{96,352},{128,384},{160,416},{192,448},{... | collective-permute-start | bytes 1572872 | tf_op jit(solution)/shard_map/ppermute | solution.py:10
  49.9 168.0 %copy-start.1 = (bf16[2,512,512]{2,1,0:T(8,128)(2,1)S(1)}, bf16[2,512,512]{2,1,0:T(8,128)(2,1)}, u32[]{:S(2)}) copy-start(bf16[2,512,512]{2,1,0:T(8,128)(2,1)} %param.6) | copy-start | bytes 3145732
  49.9 306.8 %all-reduce.7.cloned.1.call-start = ((), (), s32[]{:S(2)}) async-start(), calls=%async_computation.1 | async-start | bytes 1048576 | tf_op jit(solution)/shard_map/psum | solution.py:15
  50.9 492.4 %all-reduce.9.cloned.1.call-start = ((), (), s32[]{:S(2)}) async-start(), calls=%async_computation.2 | async-start | bytes 3145728 | tf_op jit(solution)/shard_map/psum | solution.py:15
  359.4 37.2 %collective-permute-start.1 = (bf16[512,1,512]{2,0,1:T(8,128)(2,1)S(1)}, bf16[512,1,512]{2,0,1:T(8,128)(2,1)S(1)}, u32[]{:S(2)}, u32[]{:S(2)}) collective-permute-start(bf16[512,1,512]{2,0,1:T(8,128)(2,1)S(1)} %bitcast_select_fusion.1), channel_id=1, source_target_pairs={{0,256},{32,288},{64,320},{96,352},{128,384},{160,416},{192,448},{... | collective-permute-start | bytes 1572872 | tf_op jit(solution)/shard_map/ppermute | solution.py:10
  398.2 0.8 copy-start
  398.2 145.0 %copy-start.2 = (bf16[2,512,512]{2,1,0:T(8,128)(2,1)S(1)}, bf16[2,512,512]{2,1,0:T(8,128)(2,1)}, u32[]{:S(2)}) copy-start(bf16[2,512,512]{2,1,0:T(8,128)(2,1)} %param.6) | copy-start | bytes 3145732
  398.2 283.8 %all-reduce.11.cloned.1.call-start = ((), (), s32[]{:S(2)}) async-start(), calls=%async_computation.3 | async-start | bytes 1048576 | tf_op jit(solution)/shard_map/psum | solution.py:15
Sparse Core Ops, SparseCore 0:
  50.1 167.7 all-reduce.4
  220.2 136.4 all-reduce.6
  398.4 144.8 all-reduce.8
  545.4 136.5 all-reduce.10
where the time goes:
time: 694 us; the launch traced here: 693 us
  waiting for transfers between devices  614 us (88%)
  between operations  29.7 us (4%)
  starting transfers between devices  24.1 us (3%)
  matrix products  15 us (2%)
  other arithmetic  8.07 us (1%)
    psum x4, waiting for transfers between devices, broadcast(): return lax.psum(block, axis)  572 us
    ppermute x2, waiting for transfers between devices, partner(): return lax.ppermute(value, axis, pairs)  41.7 us
    ppermute x2, starting transfers between devices, partner(): return lax.ppermute(value, axis, pairs)  24 us
  transfers between devices with their start and end apart: 6, of which 6 were waited for; matrix products, arithmetic and copies ran while one was open for 2% of the time, Pallas kernels for 0%

commit v1 on v0

v1 whole, which is shorter than its diff:
```python
import jax
import jax.numpy as jnp
from jax import lax
from jax.experimental import pallas as pl
from jax.experimental.pallas import tpu as pltpu
from jax.sharding import PartitionSpec as P

BF = jnp.bfloat16
F32 = jnp.float32
MESH = pl.DeviceIdType.MESH
PIECE = 16
CHUNK = 32
WINDOW = 2


def gather(piv, m, pn, xn, rr, sw, *scratch):
    (a1_0, a1_1, a1_2, q_0, q_1, q_2, a2_0, a2_1, a2_2, s_0, s_1, s_2, lp, w, wsrc, swsrc,
     a1_send, a1_recv, a2_send, a2_recv, g1_send, g1_recv, g1_loc, g2_send, g2_recv, g3_send, g3_recv,
     d_send, d_recv, r_send, r_edge, r_recv, r_loc, l_send, l_edge, l_recv,
     sw_send, sw_recv, w_send, w_recv, tok_up, tok_down) = scratch
    a1, q, a2, s_ = (a1_0, a1_1, a1_2), (q_0, q_1, q_2), (a2_0, a2_1, a2_2), (s_0, s_1, s_2)
    size = m.shape[1]
    half, quarter = size // 2, size // 8
    n_chunk = size // CHUNK
    z = lax.axis_index("prow")
    p = lax.axis_index("pcol")
    nz = lax.axis_size("prow")
    mid = nz // 2
    last = nz - 1
    x, y, k = p >> 3, (p >> 1) & 3, p & 1
    f, g = jnp.where(k == 0, x, y), jnp.where(k == 0, y, x)
    low = z < mid
    edge = jnp.logical_or(z == 0, z == last)
    first_one = piv[0, 1] == 0

    def dev(ff, gg):
        xx, yy = jnp.where(k == 0, ff, gg), jnp.where(k == 0, gg, ff)
        return {"pcol": xx * 8 + yy * 2 + k}

    partner = {"pcol": p ^ 1}

    def rc(src, dst, send, recv, device):
        return pltpu.make_async_remote_copy(
            src_ref=src, dst_ref=dst, send_sem=send, recv_sem=recv, device_id=device, device_id_type=MESH
        )

    def rows(start, count, align):
        return pl.ds(pl.multiple_of(start, align), count)

    barrier = pltpu.get_barrier_semaphore()
    mates = [partner]
    for t in (1, 2, 3):
        for kk in (0, 1):
            mates.append({"pcol": ((x + t) & 3) * 8 + y * 2 + kk})
            mates.append({"pcol": x * 8 + ((y + t) & 3) * 2 + kk})
    mates.append({"prow": (z + 1) & last})
    mates.append({"prow": (z + last) & last})
    for mate in mates:
        pl.semaphore_signal(barrier, inc=1, device_id=mate, device_id_type=MESH)
    pl.semaphore_wait(barrier, len(mates))

    def slot_of(o):
        return jnp.where(low, o, 2 - o)

    a1_sends = []

    def start_a1(o):
        slot = slot_of(o)
        own = pltpu.make_async_copy(
            m.at[slot, rows(k * half + f * quarter, quarter, quarter), :],
            a1[o].at[f * 2 + k], a1_recv.at[o, f * 2 + k],
        )
        own.start()
        copy = rc(
            m.at[slot, rows((1 - k) * half + g * quarter, quarter, quarter), :],
            a1[o].at[g * 2 + k], a1_send.at[o, 0], a1_recv.at[o, g * 2 + k], partner,
        )
        copy.start()
        a1_sends.append(copy)
        for t in (2, 1, 3):
            x2, y2 = (x + t) & 3, (y + t) & 3
            for n, (pos, here, target) in enumerate(
                ((x2, x, x2 * 8 + y * 2), (y2, y, x * 8 + y2 * 2 + 1))
            ):
                copy = rc(
                    m.at[slot, rows(n * half + pos * quarter, quarter, quarter), :],
                    a1[o].at[here * 2 + k], a1_send.at[o, 2 * t + n - 1],
                    a1_recv.at[o, here * 2 + k], {"pcol": target},
                )
                copy.start()
                a1_sends.append(copy)

    def finish_a1(o):
        def take(j):
            return rc(a1[o].at[j], a1[o].at[j], a1_send.at[o, 0], a1_recv.at[o, j], partner)

        pltpu.make_async_copy(a1[o].at[f * 2 + k], a1[o].at[f * 2 + k], a1_recv.at[o, f * 2 + k]).wait()
        take(f * 2 + 1 - k).wait_recv()
        for t in (1, 3, 2):
            for kk in (0, 1):
                take(((f + t) & 3) * 2 + kk).wait_recv()
        for ci in (0, 1):
            c = piv[ci, 2]
            place = jnp.where(k == 0, c >> 3, (c >> 1) & 3) * 2 + (c & 1)
            q[o][ci] = a1[o][place]

    a2_sends = []

    def start_a2(o):
        a2[o][g] = q[o][:, rows(g * PIECE, PIECE, PIECE), :]
        for t in (2, 1, 3):
            g2 = (g + t) & 3
            copy = rc(
                q[o].at[:, rows(g2 * PIECE, PIECE, PIECE), :], a2[o].at[g],
                a2_send.at[o, t - 1], a2_recv.at[o, g], dev(f, g2),
            )
            copy.start()
            a2_sends.append(copy)

    def finish_a2(o):
        for t in (1, 3, 2):
            j = (g + t) & 3
            rc(a2[o].at[j], a2[o].at[j], a2_send.at[o, 0], a2_recv.at[o, j], partner).wait_recv()
        for ci in (0, 1):
            c = piv[ci, 2]
            place = jnp.where(k == 0, (c >> 1) & 3, c >> 3)
            s_[o][ci] = a2[o][place, ci]

    base = k * half + f * quarter

    def dst(u, where):
        if u == 3:
            return xn.at[:, where, :]
        return pn.at[:, slot_of(u), where, :]

    def piece(u):
        return (w, s_[1], s_[2], lp)[u]

    def spot(ff, gg):
        return rows(k * half + ff * quarter + gg * PIECE, PIECE, PIECE)

    g_sends = []

    def start_g1(u):
        pltpu.make_async_copy(piece(u), dst(u, spot(f, g)), g1_loc.at[u]).start()
        for t in (2, 1, 3):
            copy = rc(
                piece(u), dst(u, spot(f, g)), g1_send.at[u, t - 1], g1_recv.at[u, g], dev(f, (g + t) & 3)
            )
            copy.start()
            g_sends.append(copy)

    def start_g2(u):
        pltpu.make_async_copy(piece(u), dst(u, spot(f, g)), g1_loc.at[u]).wait()
        for t in (1, 3, 2):
            j = (g + t) & 3
            rc(piece(u), dst(u, spot(f, j)), g1_send.at[u, 0], g1_recv.at[u, j], partner).wait_recv()
        for n, step in enumerate((1, 3)):
            block = dst(u, rows(base, quarter, quarter))
            copy = rc(block, block, g2_send.at[u, n], g2_recv.at[u, n], dev((f + step) & 3, g))
            copy.start()
            g_sends.append(copy)

    def start_g3(u):
        for n, step in enumerate((1, 3)):
            source = (f + 4 - step) & 3
            block = dst(u, rows(k * half + source * quarter, quarter, quarter))
            rc(block, block, g2_send.at[u, n], g2_recv.at[u, n], partner).wait_recv()
            part = dst(u, rows(k * half + source * quarter + n * (quarter // 2), quarter // 2, quarter // 2))
            copy = rc(part, part, g3_send.at[u, n], g3_recv.at[u, n], dev((f + step) & 3, g))
            copy.start()
            g_sends.append(copy)

    def start_d(u):
        across = (f + 2) & 3
        for n in (0, 1):
            part = dst(u, rows(k * half + across * quarter + n * (quarter // 2), quarter // 2, quarter // 2))
            rc(part, part, g3_send.at[u, n], g3_recv.at[u, n], partner).wait_recv()
        block = dst(u, rows(k * half, half, half))
        copy = rc(block, block, d_send.at[u], d_recv.at[u], partner)
        copy.start()
        g_sends.append(copy)

    def finish_d(u):
        block = dst(u, rows((1 - k) * half, half, half))
        rc(block, block, d_send.at[u], d_recv.at[u], partner).wait_recv()

    child = {"prow": jnp.where(low, z + 1, z - 1) & last}
    other_edge = {"prow": last - z}
    has_child = jnp.logical_and(z != mid - 1, z != mid)

    def chain_copies(b, i):
        block = rr.at[b, rows(i * CHUNK, CHUNK, CHUNK), :]
        down = rc(block, block, r_send.at[b, i], r_recv.at[b, i], child)
        over = rc(block, block, r_edge.at[i], r_recv.at[b, i], other_edge)
        return down, over

    def chain_step(i, carry):
        for b in (0, 1):
            down, over = chain_copies(b, i)
            own = z == (0 if b == 0 else last)

            @pl.when(own)
            def _():
                over.start()

            @pl.when(jnp.logical_not(own))
            def _():
                down.wait_recv()

            @pl.when(has_child)
            def _():
                down.start()

        for b in (0, 1):
            down, over = chain_copies(b, jnp.maximum(i - WINDOW, 0))
            own = z == (0 if b == 0 else last)

            @pl.when(jnp.logical_and(i >= WINDOW, has_child))
            def _():
                down.wait_send()

            @pl.when(jnp.logical_and(i >= WINDOW, own))
            def _():
                over.wait_send()

        return carry

    def chain(lo, hi):
        lax.fori_loop(lo, hi, chain_step, 0)

    def corner(b):
        down = rc(lp.at[b], lp.at[b], l_send.at[b], l_recv.at[b], child)
        over = rc(lp.at[b], lp.at[b], l_edge, l_recv.at[b], other_edge)
        return down, over

    def relay_corners():
        for b in (0, 1):
            down, over = corner(b)
            own = z == (0 if b == 0 else last)

            @pl.when(own)
            def _():
                over.start()

            @pl.when(jnp.logical_not(own))
            def _():
                down.wait_recv()

            @pl.when(has_child)
            def _():
                down.start()

    for o in (0, 1, 2):
        start_a1(o)

    @pl.when(edge)
    def _():
        b = jnp.where(z == 0, 0, 1)
        copy = pltpu.make_async_copy(m.at[jnp.where(z == 0, 0, 2)], rr.at[b], r_loc)
        copy.start()
        copy.wait()

    give = jnp.logical_or(z == mid, z == mid - 1)
    slot_a = jnp.where(jnp.logical_xor(z == mid, first_one), piv[1, 0], piv[0, 0]) >> 4

    @pl.when(z == 0)
    def _():
        pl.semaphore_signal(tok_up, inc=1, device_id={"prow": z + 1}, device_id_type=MESH)

    @pl.when(z == last)
    def _():
        pl.semaphore_signal(tok_down, inc=1, device_id={"prow": z - 1}, device_id_type=MESH)

    @pl.when(jnp.logical_and(z >= 1, z <= mid))
    def _():
        pl.semaphore_wait(tok_up, 1)

    @pl.when(jnp.logical_and(z >= 1, z < mid))
    def _():
        pl.semaphore_signal(tok_up, inc=1, device_id={"prow": z + 1}, device_id_type=MESH)

    @pl.when(jnp.logical_and(z >= mid - 1, z < last))
    def _():
        pl.semaphore_wait(tok_down, 1)

    @pl.when(jnp.logical_and(z >= mid, z < last))
    def _():
        pl.semaphore_signal(tok_down, inc=1, device_id={"prow": z - 1}, device_id_type=MESH)

    receiver = {"prow": jnp.where(z == mid, 0, last)}
    sw_copy = rc(swsrc, sw, sw_send, sw_recv, receiver)
    w_copy = rc(wsrc, w, w_send, w_recv, receiver)

    @pl.when(give)
    def _():
        swsrc[...] = m[slot_a]
        sw_copy.start()

    far = jnp.where(low, z, last - z)

    def at(us):
        return jnp.clip((us * 10 - far * 14) // 14, 0, n_chunk)

    marks = [at(us) for us in (5, 8, 11, 14, 17)]
    chain(0, marks[0])
    finish_a1(0)
    start_a2(0)
    chain(marks[0], marks[1])
    finish_a1(1)
    start_a2(1)
    finish_a2(0)

    @pl.when(edge)
    def _():
        which = jnp.where(jnp.logical_xor(z == 0, first_one), 0, 1)
        lp[jnp.where(z == 0, 0, 1)] = s_[0][which]

    chain(marks[1], marks[2])
    finish_a1(2)
    start_a2(2)
    finish_a2(1)
    start_g1(1)

    @pl.when(jnp.logical_not(give))
    def _():
        relay_corners()

    chain(marks[2], marks[3])
    finish_a2(2)
    start_g1(2)

    @pl.when(give)
    def _():
        order_a = jnp.where(z == mid, 2 - slot_a, slot_a)
        value = jnp.where(order_a == 1, s_[1][...], s_[0][...])
        wsrc[...] = jnp.where(order_a == 2, s_[2][...], value)
        w_copy.start()

    @pl.when(give)
    def _():
        relay_corners()

    start_g2(1)
    start_g1(3)
    chain(marks[3], marks[4])
    start_g2(2)
    start_g3(1)

    @pl.when(edge)
    def _():
        w_copy.wait_recv()

    @pl.when(jnp.logical_not(edge))
    def _():
        w[...] = s_[0][...]

    start_g1(0)
    start_g2(3)
    start_g3(2)
    start_d(1)
    start_g2(0)
    start_g3(3)
    start_d(2)
    start_g3(0)
    start_d(3)
    chain(marks[4], n_chunk)
    start_d(0)
    for u in (1, 2, 3, 0):
        finish_d(u)

    @pl.when(edge)
    def _():
        sw_copy.wait_recv()

    @pl.when(give)
    def _():
        sw_copy.wait_send()
        w_copy.wait_send()

    for copy in a1_sends + a2_sends + g_sends:
        copy.wait_send()
    for b in (0, 1):
        own = z == (0 if b == 0 else last)
        down, over = corner(b)

        @pl.when(has_child)
        def _():
            down.wait_send()
            for i in range(n_chunk - WINDOW, n_chunk):
                chain_copies(b, i)[0].wait_send()

        @pl.when(own)
        def _():
            over.wait_send()
            for i in range(n_chunk - WINDOW, n_chunk):
                chain_copies(b, i)[1].wait_send()


def run_gather(pivots, blocks):
    slots, size, width = blocks.shape
    n_chunk = size // CHUNK
    quarter = size // 8
    vm = pltpu.VMEM
    dma = pltpu.SemaphoreType.DMA
    scratch = (
        [vm((8, quarter, width), BF)] * 3
        + [vm((2, quarter, width), BF)] * 3
        + [vm((4, 2, PIECE, width), BF)] * 3
        + [vm((2, PIECE, width), BF)] * 6
        + [vm((size, width), BF)]
        + [dma((3, 8)), dma((3, 8)), dma((3, 3)), dma((3, 4)), dma((4, 3)), dma((4, 4)), dma((4,))]
        + [dma((4, 2)), dma((4, 2)), dma((4, 2)), dma((4, 2)), dma((4,)), dma((4,))]
        + [dma((2, n_chunk)), dma((n_chunk,)), dma((2, n_chunk)), dma(())]
        + [dma((2,)), dma(()), dma((2,))]
        + [dma(())] * 4
        + [pltpu.SemaphoreType.REGULAR] * 2
    )
    return pl.pallas_call(
        gather,
        out_shape=[
            jax.ShapeDtypeStruct((2, slots, size, width), BF),
            jax.ShapeDtypeStruct((2, size, width), BF),
            jax.ShapeDtypeStruct((2, size, width), BF),
            jax.ShapeDtypeStruct((size, width), BF),
        ],
        in_specs=[pl.BlockSpec(memory_space=pltpu.SMEM), pl.BlockSpec(memory_space=pltpu.VMEM)],
        out_specs=[pl.BlockSpec(memory_space=pltpu.VMEM)] * 4,
        scratch_shapes=scratch,
        compiler_params=pltpu.CompilerParams(collective_id=0, has_side_effects=True),
        name="gather",
    )(pivots, blocks)


def local(matrix, pattern, inverses, pivots):
    nrow = lax.axis_size("prow")
    slots, size, _, width = matrix.shape
    my_row = lax.axis_index("prow")
    my_col = lax.axis_index("pcol")
    blocks = matrix.reshape(slots, size, width)
    panels, corners, tops, swapped = run_gather(pivots, blocks)
    a1, b1, c1 = pivots[0, 0], pivots[0, 1], pivots[0, 2]
    a2, b2, c2 = pivots[1, 0], pivots[1, 1], pivots[1, 2]
    low_first = b1 == 0
    ids = jnp.arange(slots, dtype=jnp.int32) * nrow + my_row
    held = jnp.where(ids == b1, a1, jnp.where(ids == b2, a2, ids))
    taken = ids != held
    keep = pattern.astype(BF)
    work = jnp.where(taken[:, None, None], swapped[None], blocks) * keep[held, my_col][:, None, None]
    panel1 = panels[0] * keep[held, c1][:, None, None]
    panel2 = panels[1] * keep[held, c2][:, None, None]
    corner12 = jnp.where(low_first, corners[0], corners[1]) * keep[b1, c2]
    corner21 = jnp.where(low_first, corners[1], corners[0]) * keep[b2, c1]
    upper1 = jnp.where(low_first, tops[0], tops[1]) * keep[b1, my_col]
    raw2 = jnp.where(low_first, tops[1], tops[0]) * keep[b2, my_col]

    def dot(left, right):
        return jnp.dot(left, right, preferred_element_type=F32)

    def less(old, left, right):
        return (old.astype(F32) - dot(left, right)).astype(BF)

    flat = (slots * size, width)
    left1 = dot(panel1.reshape(flat), inverses[0]).astype(BF)
    top_left = dot(corner21, inverses[0]).astype(BF)
    upper2 = jnp.where(my_col == c1, top_left, less(raw2, top_left, upper1))
    step1 = less(work.reshape(flat), left1, upper1)
    panel2 = less(panel2.reshape(flat), left1, corner12)
    left2 = dot(panel2, inverses[1]).astype(BF)
    step2 = less(step1, left2, upper2)
    mixed = jnp.where(my_col == c1, left1, jnp.where(my_col == c2, left2, step2)).reshape(blocks.shape)
    is1, is2 = (ids == a1)[:, None, None], (ids == a2)[:, None, None]
    out = jnp.where(is1, upper1[None], jnp.where(is2, upper2[None], mixed))
    return out.reshape(matrix.shape)


def solution(mesh):
    placed = (P(None, "prow", None, "pcol"), P(), P(), P())
    return jax.shard_map(
        local, mesh=mesh, in_specs=placed, out_specs=P(None, "prow", None, "pcol"), check_vma=False
    )
```

time: 694 us -> 217 us (0.31)
  the two profiles are of different devices: /device:TPU:6 before, /device:TPU:225 now
where the time goes in v1:
time: 217 us; the launch traced here: 216 us
  Pallas kernels  175 us (81%)
  matrix products  13.4 us (6%)
  other arithmetic  11.3 us (5%)
  between operations  9.69 us (4%)
  local copies, waits for them, and re-layouts  6.93 us (3%)
    pallas_call x1, Pallas kernels, run_gather(): pl.pallas_call(gather, out_shape=[jax.ShapeDtypeStruct((2, slots, size, w...  175 us
    dot_general x6, matrix products, dot(): return jnp.dot(left, right, preferred_element_type=F32)  13.4 us

profile of v1, /device:TPU:225, one launch (start us, length us, event | category | flops | bytes accessed | tf_op | source)
XLA Modules:
  0.0 216.1 jit_solution(2638913977547747164)
XLA Ops:
  0.0 1.6 fusion.41
  11.1 0.6 broadcast_compare_fusion.1
  11.8 2.5 %or_bitcast_fusion = (s32[3]{0:T(128)S(1)}, s32[3,1]{0,1:T(1,128)S(1)}) fusion(s32[]{:T(128)S(6)} %shift-left.8, s32[]{:T(128)} %bitcast.5, s32[]{:T(128)} %bitcast.7, s32[]{:T(128)} %bitcast, s32[]{:T(128)} %bitcast.1, s32[]{:T(128)S(6)} %axis_index.23), kind=kLoop, calls=%fused_computation.51 | loop fusion | flops 36 | bytes 48 | tf_op jit(solution)/shard_map/concatenate | solution.py:449
  14.2 2.5 %fusion.35 = (pred[3]{0:T(512)(128)(4,1)S(1)}, pred[3]{0:T(512)(128)(4,1)S(1)}) fusion(s32[]{:T(128)} %bitcast.7, s32[]{:T(128)} %bitcast.1, s32[]{:T(128)} %bitcast.5, s32[]{:T(128)} %bitcast, s32[]{:T(128)S(6)} %axis_index.23), kind=kLoop, calls=%fused_computation.48 | loop fusion | flops 24 | bytes 26 | tf_op jit(solution)/shard_map/ne | solution.py:447
  16.7 0.1 broadcast_in_dim.67
  16.8 0.7 convert_element_type.39
  17.5 0.6 fusion.40
  18.1 0.7 gather_fusion
  18.8 0.7 gather_fusion.2
  19.4 0.7 gather_fusion.1
  20.1 0.1 mul.105
  20.2 0.1 mul.112
  20.3 174.9 %gather.16 = (bf16[2,3,512,512]{3,2,1,0:T(8,128)(2,1)}, bf16[2,512,512]{2,1,0:T(8,128)(2,1)}, bf16[2,512,512]{2,1,0:T(8,128)(2,1)}, bf16[512,512]{1,0:T(8,128)(2,1)}) custom-call(s32[2,3]{1,0:T(2,128)} %piv.1, bf16[3,512,512]{2,1,0:T(8,128)(2,1)} %bitcast.57), custom_call_target="tpu_custom_call" | custom-call | tf_op jit(solution)/shard_map/gather/pallas_call | solution.py:419
  195.2 2.1 fusion.39
  197.3 0.0 copy-start.3
  197.3 0.3 bitcast_multiply_fusion
  197.6 0.9 copy-done.3
  198.5 2.1 convolution_convert_fusion.1
  200.7 5.3 %convolution_convert_fusion = bf16[1536,512]{1,0:T(8,128)(2,1)} fusion(bf16[1536,512]{1,0:T(8,128)(2,1)} %convolution_convert_fusion.1, bf16[1536,512]{1,0:T(8,128)(2,1)S(1)} %bitcast_multiply_fusion, bf16[2,512,512]{2,1,0:T(8,128)(2,1)S(1)} %copy-done.3, pred[]{:T(512)S(6)} %eq.78, bf16[2,512,512]{2,1,0:T(8,128)(2,1)} %get-tuple-element.10, bf16[]{:T(256)} %bitcast.18), kind=kOutput, calls=%fused_computation.6 | convolution fusion | flops 1614282752 | bytes 6291459 | tf_op jit(solution)/shard_map/dot_general | solution.py:458
  206.0 0.0 copy-start.1
  206.0 2.4 %convolution_convert_fusion.2 = bf16[512,512]{1,0:T(8,128)(2,1)S(1)} fusion(pred[]{:T(512)S(6)} %eq.78, bf16[2,512,512]{2,1,0:T(8,128)(2,1)S(1)} %copy-done.3, bf16[2,512,512]{2,1,0:T(8,128)(2,1)} %get-tuple-element.10, bf16[]{:T(256)} %bitcast.8), kind=kOutput, calls=%fused_computation.19 | convolution fusion | flops 269221888 | bytes 2097155 | tf_op jit(solution)/shard_map/dot_general | solution.py:458
  208.3 0.0 copy-done.1
  208.3 0.7 multiply_bitcast_fusion
  209.0 0.0 copy-start
  209.0 0.0 copy-start.2
  209.0 1.2 fusion.7
  210.2 0.2 copy-done
  210.4 0.1 copy-done.2
  210.5 0.0 copy-start.4
  210.5 0.5 fusion.5
  211.1 0.9 copy-done.4
  211.9 0.0 copy-start.5
  211.9 1.0 fusion.1
  213.0 0.4 copy-done.5
  213.3 1.4 fusion.4
  214.7 1.4 select_select_fusion
  (4 shorter events, 0.1 us)
Async XLA Ops:
  197.3 1.2 copy-start.3
  206.0 2.4 %copy-start.1 = (bf16[2,512,512]{2,1,0:T(8,128)(2,1)S(1)}, bf16[2,512,512]{2,1,0:T(8,128)(2,1)}, u32[]{:S(2)}) copy-start(bf16[2,512,512]{2,1,0:T(8,128)(2,1)} %get-tuple-element.9) | copy-start | bytes 3145732
  209.0 1.4 copy-start
  209.0 1.5 copy-start.2
  210.5 1.4 copy-start.4
  211.9 1.4 copy-start.5

commit v2 on v1

v2 whole, which is shorter than its diff:
```python
import jax
import jax.numpy as jnp
from jax import lax
from jax.experimental import pallas as pl
from jax.experimental.pallas import tpu as pltpu
from jax.sharding import PartitionSpec as P

BF = jnp.bfloat16
F32 = jnp.float32
MESH = pl.DeviceIdType.MESH
PIECE = 16
CHUNK = 32


def gather(piv, m, pn, xn, rr, sw, *scratch):
    (a1_0, a1_1, a1_2, q_0, q_1, q_2, a2_0, a2_1, a2_2, s_0, s_1, s_2, lp, w, wsrc, swsrc,
     a1_send, a1_recv, a2_send, a2_recv, g1_send, g1_recv, g1_loc, g2_send, g2_recv,
     d_send, d_recv, r_send, r_recv, r_loc, l_send, l_recv,
     sw_send, sw_recv, w_send, w_recv, tok_up, tok_down, tok_in, tok_over) = scratch
    a1, q, a2, s_ = (a1_0, a1_1, a1_2), (q_0, q_1, q_2), (a2_0, a2_1, a2_2), (s_0, s_1, s_2)
    size = m.shape[1]
    half, quarter = size // 2, size // 8
    n_chunk = size // CHUNK
    z = lax.axis_index("prow")
    p = lax.axis_index("pcol")
    nz = lax.axis_size("prow")
    mid = nz // 2
    last = nz - 1
    x, y, k = p >> 3, (p >> 1) & 3, p & 1
    f, g = jnp.where(k == 0, x, y), jnp.where(k == 0, y, x)
    low = z < mid
    edge = jnp.logical_or(z == 0, z == last)
    first_one = piv[0, 1] == 0

    def dev(ff, gg):
        xx, yy = jnp.where(k == 0, ff, gg), jnp.where(k == 0, gg, ff)
        return {"pcol": xx * 8 + yy * 2 + k}

    partner = {"pcol": p ^ 1}

    def rc(src, dst, send, recv, device):
        return pltpu.make_async_remote_copy(
            src_ref=src, dst_ref=dst, send_sem=send, recv_sem=recv, device_id=device, device_id_type=MESH
        )

    def rows(start, count, align):
        return pl.ds(pl.multiple_of(start, align), count)

    barrier = pltpu.get_barrier_semaphore()
    mates = [partner]
    for t in (1, 2, 3):
        for kk in (0, 1):
            mates.append({"pcol": ((x + t) & 3) * 8 + y * 2 + kk})
            mates.append({"pcol": x * 8 + ((y + t) & 3) * 2 + kk})
    mates.append({"prow": (z + 1) & last})
    mates.append({"prow": (z + last) & last})
    for mate in mates:
        pl.semaphore_signal(barrier, inc=1, device_id=mate, device_id_type=MESH)
    hub = mid // 2

    @pl.when(jnp.logical_or(z == hub, z == last - hub))
    def _():
        for at in (0, last):
            pl.semaphore_signal(barrier, inc=1, device_id={"prow": at}, device_id_type=MESH)

    pl.semaphore_wait(barrier, jnp.where(edge, len(mates) + 2, len(mates)))

    def slot_of(o):
        return jnp.where(low, o, 2 - o)

    a1_sends = []

    def start_a1(o):
        slot = slot_of(o)
        own = pltpu.make_async_copy(
            m.at[slot, rows(k * half + f * quarter, quarter, quarter), :],
            a1[o].at[f * 2 + k], a1_recv.at[o, f * 2 + k],
        )
        own.start()
        copy = rc(
            m.at[slot, rows((1 - k) * half + g * quarter, quarter, quarter), :],
            a1[o].at[g * 2 + k], a1_send.at[o, 0], a1_recv.at[o, g * 2 + k], partner,
        )
        copy.start()
        a1_sends.append(copy)
        for t in (2, 1, 3):
            x2, y2 = (x + t) & 3, (y + t) & 3
            for n, (pos, here, target) in enumerate(
                ((x2, x, x2 * 8 + y * 2), (y2, y, x * 8 + y2 * 2 + 1))
            ):
                copy = rc(
                    m.at[slot, rows(n * half + pos * quarter, quarter, quarter), :],
                    a1[o].at[here * 2 + k], a1_send.at[o, 2 * t + n - 1],
                    a1_recv.at[o, here * 2 + k], {"pcol": target},
                )
                copy.start()
                a1_sends.append(copy)

    def finish_a1(o):
        def take(j):
            return rc(a1[o].at[j], a1[o].at[j], a1_send.at[o, 0], a1_recv.at[o, j], partner)

        pltpu.make_async_copy(a1[o].at[f * 2 + k], a1[o].at[f * 2 + k], a1_recv.at[o, f * 2 + k]).wait()
        take(f * 2 + 1 - k).wait_recv()
        for t in (1, 3, 2):
            for kk in (0, 1):
                take(((f + t) & 3) * 2 + kk).wait_recv()
        for ci in (0, 1):
            c = piv[ci, 2]
            place = jnp.where(k == 0, c >> 3, (c >> 1) & 3) * 2 + (c & 1)
            q[o][ci] = a1[o][place]

    a2_sends = []

    def start_a2(o):
        a2[o][g] = q[o][:, rows(g * PIECE, PIECE, PIECE), :]
        for t in (2, 1, 3):
            g2 = (g + t) & 3
            copy = rc(
                q[o].at[:, rows(g2 * PIECE, PIECE, PIECE), :], a2[o].at[g],
                a2_send.at[o, t - 1], a2_recv.at[o, g], dev(f, g2),
            )
            copy.start()
            a2_sends.append(copy)

    def finish_a2(o):
        for t in (1, 3, 2):
            j = (g + t) & 3
            rc(a2[o].at[j], a2[o].at[j], a2_send.at[o, 0], a2_recv.at[o, j], partner).wait_recv()
        for ci in (0, 1):
            c = piv[ci, 2]
            place = jnp.where(k == 0, (c >> 1) & 3, c >> 3)
            s_[o][ci] = a2[o][place, ci]

    base = k * half + f * quarter

    def dst(u, where):
        if u == 3:
            return xn.at[:, where, :]
        return pn.at[:, slot_of(u), where, :]

    def piece(u):
        return (w, s_[1], s_[2], lp)[u]

    def spot(ff, gg):
        return rows(k * half + ff * quarter + gg * PIECE, PIECE, PIECE)

    g_sends = []

    def start_g1(u):
        pltpu.make_async_copy(piece(u), dst(u, spot(f, g)), g1_loc.at[u]).start()
        for t in (2, 1, 3):
            copy = rc(
                piece(u), dst(u, spot(f, g)), g1_send.at[u, t - 1], g1_recv.at[u, g], dev(f, (g + t) & 3)
            )
            copy.start()
            g_sends.append(copy)

    def start_g2(u):
        pltpu.make_async_copy(piece(u), dst(u, spot(f, g)), g1_loc.at[u]).wait()
        for t in (1, 3, 2):
            j = (g + t) & 3
            rc(piece(u), dst(u, spot(f, j)), g1_send.at[u, 0], g1_recv.at[u, j], partner).wait_recv()
        block = dst(u, rows(base, quarter, quarter))
        for t in (2, 1, 3):
            copy = rc(block, block, g2_send.at[u, t - 1], g2_recv.at[u, f], dev((f + t) & 3, g))
            copy.start()
            g_sends.append(copy)

    def start_d(u):
        for t in (1, 3, 2):
            j = (f + t) & 3
            block = dst(u, rows(k * half + j * quarter, quarter, quarter))
            rc(block, block, g2_send.at[u, 0], g2_recv.at[u, j], partner).wait_recv()
        block = dst(u, rows(k * half, half, half))
        copy = rc(block, block, d_send.at[u], d_recv.at[u], partner)
        copy.start()
        g_sends.append(copy)

    def finish_d(u):
        block = dst(u, rows((1 - k) * half, half, half))
        rc(block, block, d_send.at[u], d_recv.at[u], partner).wait_recv()

    h = jnp.where(low, z, last - z)

    def at_height(height):
        return {"prow": jnp.where(low, height, last - height) & last}

    other_edge = {"prow": last - z}
    relays = jnp.logical_and(h >= 2, h <= mid - 2)
    sinks = jnp.logical_and(h >= 2, h <= hub)
    rises = jnp.logical_and(h >= hub, h <= mid - 2)

    def row_chunk(b, i, n, device):
        block = rr.at[b, rows(i * CHUNK, CHUNK, CHUNK), :]
        return rc(block, block, r_send.at[n, b, i], r_recv.at[b, i], device)

    def source_copies(b, i):
        return (
            row_chunk(b, i, 0, {"prow": hub}),
            row_chunk(b, i, 1, {"prow": last - hub}),
            row_chunk(b, i, 2, other_edge),
        )

    def relay_step(i, carry):
        for b in (0, 1):
            fall, rise = row_chunk(b, i, 0, at_height(h - 1)), row_chunk(b, i, 1, at_height(h + 1))
            fall.wait_recv()

            @pl.when(sinks)
            def _():
                fall.start()

            @pl.when(rises)
            def _():
                rise.start()

        return carry

    def chain(lo, hi):
        lax.fori_loop(lo, hi, relay_step, 0)

    def corner(b, t):
        return rc(lp.at[b], lp.at[b], l_send.at[t - 1], l_recv.at[b], {"prow": (z + t) & last})

    for o in (0, 1, 2):
        start_a1(o)

    for b, at in ((0, 0), (1, last)):

        @pl.when(z == at)
        def _():
            copy = pltpu.make_async_copy(m.at[0 if b == 0 else 2], rr.at[b], r_loc)
            copy.start()
            copy.wait()

            def send(i, carry):
                for copy in source_copies(b, i):
                    copy.start()
                return carry

            lax.fori_loop(0, n_chunk, send, 0)

    give = jnp.logical_or(z == mid, z == mid - 1)
    slot_a = jnp.where(jnp.logical_xor(z == mid, first_one), piv[1, 0], piv[0, 0]) >> 4

    @pl.when(z == 0)
    def _():
        pl.semaphore_signal(tok_up, inc=1, device_id={"prow": z + 1}, device_id_type=MESH)

    @pl.when(z == last)
    def _():
        pl.semaphore_signal(tok_down, inc=1, device_id={"prow": z - 1}, device_id_type=MESH)

    @pl.when(jnp.logical_and(z >= 1, z <= mid))
    def _():
        pl.semaphore_wait(tok_up, 1)

    @pl.when(jnp.logical_and(z >= 1, z < mid))
    def _():
        pl.semaphore_signal(tok_up, inc=1, device_id={"prow": z + 1}, device_id_type=MESH)

    @pl.when(jnp.logical_and(z >= mid - 1, z < last))
    def _():
        pl.semaphore_wait(tok_down, 1)

    @pl.when(jnp.logical_and(z >= mid, z < last))
    def _():
        pl.semaphore_signal(tok_down, inc=1, device_id={"prow": z - 1}, device_id_type=MESH)

    receiver = {"prow": jnp.where(z == mid, 0, last)}
    sw_copy = rc(swsrc, sw, sw_send, sw_recv, receiver)
    w_copy = rc(wsrc, w, w_send, w_recv, receiver)

    @pl.when(give)
    def _():
        swsrc[...] = m[slot_a]
        sw_copy.start()

    begin = 90 + 33 * jnp.abs(h - hub)

    def mark(us):
        return jnp.where(relays, jnp.clip(jnp.maximum(us * 10 - begin, 0) // 12, 0, n_chunk), 0)

    marks = [mark(us) for us in (9, 12, 14, 18, 20, 22, 25, 27, 29, 33)]
    done = [0]

    def relay_to(n):
        chain(done[-1], marks[n])
        done.append(marks[n])

    relay_to(0)
    finish_a1(0)
    start_a2(0)

    @pl.when(jnp.logical_and(h >= 1, h < mid - 1))
    def _():
        pl.semaphore_wait(tok_in, 1)

    @pl.when(h >= 1)
    def _():
        pl.semaphore_signal(tok_in, inc=1, device_id=at_height(h - 1), device_id_type=MESH)

    relay_to(1)
    finish_a1(1)
    start_a2(1)
    finish_a2(0)

    @pl.when(edge)
    def _():
        which = jnp.where(jnp.logical_xor(z == 0, first_one), 0, 1)
        lp[jnp.where(z == 0, 0, 1)] = s_[0][which]
        pl.semaphore_wait(tok_in, 1)
        pl.semaphore_signal(tok_over, inc=1, device_id=other_edge, device_id_type=MESH)
        pl.semaphore_wait(tok_over, 1)

    for b, at in ((0, 0), (1, last)):

        @pl.when(z == at)
        def _():
            for t in (8, 7, 9, 6, 10, 5, 11, 4, 12, 3, 13, 2, 14, 1, 15):
                corner(b, t).start()

    relay_to(2)
    finish_a1(2)
    start_a2(2)
    finish_a2(1)
    start_g1(1)
    relay_to(3)
    finish_a2(2)

    @pl.when(give)
    def _():
        order_a = jnp.where(z == mid, 2 - slot_a, slot_a)
        value = jnp.where(order_a == 1, s_[1][...], s_[0][...])
        wsrc[...] = jnp.where(order_a == 2, s_[2][...], value)
        w_copy.start()

    start_g1(2)
    relay_to(4)
    start_g2(1)
    relay_to(5)
    for b, at in ((0, 0), (1, last)):

        @pl.when(z != at)
        def _():
            corner(b, 1).wait_recv()

    start_g1(3)
    start_g2(2)
    relay_to(6)
    start_d(1)
    relay_to(7)

    @pl.when(edge)
    def _():
        w_copy.wait_recv()

    @pl.when(jnp.logical_not(edge))
    def _():
        w[...] = s_[0][...]

    start_g1(0)
    start_g2(3)
    relay_to(8)
    start_d(2)
    start_g2(0)
    relay_to(9)
    start_d(3)
    chain(done[-1], jnp.where(relays, n_chunk, 0))
    start_d(0)
    for u in (1, 2, 3, 0):
        finish_d(u)

    @pl.when(edge)
    def _():
        sw_copy.wait_recv()

    def leaf(i, carry):
        for b, at in ((0, 0), (1, last)):

            @pl.when(z != at)
            def _():
                row_chunk(b, i, 0, other_edge).wait_recv()

        return carry

    lax.fori_loop(0, jnp.where(relays, 0, n_chunk), leaf, 0)

    @pl.when(give)
    def _():
        sw_copy.wait_send()
        w_copy.wait_send()

    for copy in a1_sends + a2_sends + g_sends:
        copy.wait_send()

    for b, at in ((0, 0), (1, last)):

        @pl.when(z == at)
        def _():
            for t in range(1, 16):
                corner(b, t).wait_send()

            def sent(i, carry):
                for copy in source_copies(b, i):
                    copy.wait_send()
                return carry

            lax.fori_loop(0, n_chunk, sent, 0)

    def relayed(i, carry):
        for b in (0, 1):

            @pl.when(sinks)
            def _():
                row_chunk(b, i, 0, other_edge).wait_send()

            @pl.when(rises)
            def _():
                row_chunk(b, i, 1, other_edge).wait_send()

        return carry

    lax.fori_loop(0, jnp.where(relays, n_chunk, 0), relayed, 0)


def run_gather(pivots, blocks):
    slots, size, width = blocks.shape
    n_chunk = size // CHUNK
    quarter = size // 8
    vm = pltpu.VMEM
    dma = pltpu.SemaphoreType.DMA
    scratch = (
        [vm((8, quarter, width), BF)] * 3
        + [vm((2, quarter, width), BF)] * 3
        + [vm((4, 2, PIECE, width), BF)] * 3
        + [vm((2, PIECE, width), BF)] * 6
        + [vm((size, width), BF)]
        + [dma((3, 8)), dma((3, 8)), dma((3, 3)), dma((3, 4)), dma((4, 3)), dma((4, 4)), dma((4,))]
        + [dma((4, 3)), dma((4, 4)), dma((4,)), dma((4,))]
        + [dma((3, 2, n_chunk)), dma((2, n_chunk)), dma(())]
        + [dma((15,)), dma((2,))]
        + [dma(())] * 4
        + [pltpu.SemaphoreType.REGULAR] * 4
    )
    return pl.pallas_call(
        gather,
        out_shape=[
            jax.ShapeDtypeStruct((2, slots, size, width), BF),
            jax.ShapeDtypeStruct((2, size, width), BF),
            jax.ShapeDtypeStruct((2, size, width), BF),
            jax.ShapeDtypeStruct((size, width), BF),
        ],
        in_specs=[pl.BlockSpec(memory_space=pltpu.SMEM), pl.BlockSpec(memory_space=pltpu.VMEM)],
        out_specs=[pl.BlockSpec(memory_space=pltpu.VMEM)] * 4,
        scratch_shapes=scratch,
        compiler_params=pltpu.CompilerParams(collective_id=0, has_side_effects=True),
        name="gather",
    )(pivots, blocks)


def update(piv, pat, blocks, panels, corners, tops, swapped, inv, out, lead, upper):
    slots, size, width = blocks.shape
    row = lax.axis_index("prow")
    col = lax.axis_index("pcol")
    nrow = lax.axis_size("prow")
    a1, b1, c1 = piv[0, 0], piv[0, 1], piv[0, 2]
    a2, b2, c2 = piv[1, 0], piv[1, 1], piv[1, 2]
    one = jnp.where(b1 == 0, 0, 1)
    two = 1 - one

    def keep(i, j):
        return pat[i, j].astype(F32)

    def dot(left, right):
        return jnp.dot(left, right, preferred_element_type=F32)

    own1 = keep(b1, col)
    cross12 = keep(b1, c2)
    lead[...] = (dot(corners[two], inv[0]) * keep(b2, c1)).astype(BF)

    @pl.when(col == c1)
    def _():
        upper[...] = lead[...]

    @pl.when(col != c1)
    def _():
        old = tops[two].astype(F32) * keep(b2, col)
        upper[...] = (old - dot(lead[...], tops[one]) * own1).astype(BF)

    def slot(s, carry):
        here = s * nrow + row
        held = jnp.where(here == b1, a1, jnp.where(here == b2, a2, here))
        old = jnp.where(here == held, blocks[s], swapped[...]).astype(F32) * keep(held, col)
        left1 = (dot(panels[0, s], inv[0]) * keep(held, c1)).astype(BF)
        step1 = (old - dot(left1, tops[one]) * own1).astype(BF)
        column2 = panels[1, s].astype(F32) * keep(held, c2) - dot(left1, corners[one]) * cross12
        left2 = dot(column2.astype(BF), inv[1]).astype(BF)
        out[s] = (step1.astype(F32) - dot(left2, upper[...])).astype(BF)

        @pl.when(col == c1)
        def _():
            out[s] = left1

        @pl.when(col == c2)
        def _():
            out[s] = left2

        @pl.when(here == a1)
        def _():
            out[s] = (tops[one].astype(F32) * own1).astype(BF)

        @pl.when(here == a2)
        def _():
            out[s] = upper[...]

        return carry

    lax.fori_loop(0, slots, slot, 0)


def run_update(pivots, pattern, blocks, panels, corners, tops, swapped, inverses):
    slots, size, width = blocks.shape
    smem, vmem = pl.BlockSpec(memory_space=pltpu.SMEM), pl.BlockSpec(memory_space=pltpu.VMEM)
    return pl.pallas_call(
        update,
        out_shape=jax.ShapeDtypeStruct(blocks.shape, BF),
        in_specs=[smem, smem] + [vmem] * 6,
        out_specs=vmem,
        scratch_shapes=[pltpu.VMEM((size, width), BF)] * 2,
        name="update",
    )(pivots, pattern, blocks, panels, corners, tops, swapped, inverses)


def local(matrix, pattern, inverses, pivots):
    slots, size, _, width = matrix.shape
    blocks = matrix.reshape(slots, size, width)
    moved = run_gather(pivots, blocks)
    return run_update(pivots, pattern, blocks, *moved, inverses).reshape(matrix.shape)


def solution(mesh):
    placed = (P(None, "prow", None, "pcol"), P(), P(), P())
    return jax.shard_map(
        local, mesh=mesh, in_specs=placed, out_specs=P(None, "prow", None, "pcol"), check_vma=False
    )
```

time: 217 us -> 91 us (0.42)
  the two profiles are of different devices: /device:TPU:225 before, /device:TPU:34 now
where the time goes in v2:
time: 91 us; the launch traced here: 90.8 us
  Pallas kernels  89.3 us (98%)
  local copies, waits for them, and re-layouts  1.41 us (2%)
    pallas_call x1, Pallas kernels, run_gather(): pl.pallas_call(gather, out_shape=[jax.ShapeDtypeStruct((2, slots, size, w...  79.3 us
    pallas_call x1, Pallas kernels, run_update(): pl.pallas_call(update, out_shape=jax.ShapeDtypeStruct(blocks.shape, BF),...  10.1 us

profile of v2, /device:TPU:34, one launch (start us, length us, event | category | flops | bytes accessed | tf_op | source)
XLA Modules:
  0.0 90.8 jit_solution(17852162546239236521)
XLA Ops:
  0.0 1.4 %copy.5.pat = s32[48,32]{1,0:T(8,128)} copy(s32[48,32]{0,1:T(8,128)} %param.5) | data formatting | bytes 12288 | tf_op args[1]
  1.4 79.3 %gather.1 = (bf16[2,3,512,512]{3,2,1,0:T(8,128)(2,1)}, bf16[2,512,512]{2,1,0:T(8,128)(2,1)}, bf16[2,512,512]{2,1,0:T(8,128)(2,1)}, bf16[512,512]{1,0:T(8,128)(2,1)}) custom-call(s32[2,3]{1,0:T(2,128)} %piv.3, bf16[3,512,512]{2,1,0:T(8,128)(2,1)} %bitcast.4), custom_call_target="tpu_custom_call" | custom-call | tf_op jit(solution)/shard_map/gather/pallas_call | solution.py:447
  80.7 10.1 %update.1 = bf16[3,512,512]{2,1,0:T(8,128)(2,1)} custom-call(s32[2,3]{1,0:T(2,128)} %piv.3, s32[48,32]{1,0:T(8,128)} %copy.5.pat, bf16[3,512,512]{2,1,0:T(8,128)(2,1)} %bitcast.5, bf16[2,3,512,512]{3,2,1,0:T(8,128)(2,1)} %get-tuple-element.9.panels, bf16[2,512,512]{2,1,0:T(8,128)(2,1)} %get-tuple-element.10.corners, ...), custom_call_target="tpu_custom_call" | custom-call | tf_op jit(solution)/shard_map/update/pallas_call | solution.py:526

commit v3 on v2

--- a/solution.py
+++ b/solution.py
@@ -10,13 +10,14 @@
 MESH = pl.DeviceIdType.MESH
 PIECE = 16
 CHUNK = 32
+FIRST = 8
 
 
 def gather(piv, m, pn, xn, rr, sw, *scratch):
-    (a1_0, a1_1, a1_2, q_0, q_1, q_2, a2_0, a2_1, a2_2, s_0, s_1, s_2, lp, w, wsrc, swsrc,
+    (a1_0, a1_1, a1_2, q_0, q_1, q_2, a2_0, a2_1, a2_2, s_0, s_1, s_2, lp, w, mp,
      a1_send, a1_recv, a2_send, a2_recv, g1_send, g1_recv, g1_loc, g2_send, g2_recv,
      d_send, d_recv, r_send, r_recv, r_loc, l_send, l_recv,
-     sw_send, sw_recv, w_send, w_recv, tok_up, tok_down, tok_in, tok_over) = scratch
+     sw_send, sw_recv, w_send, w_recv, tok_in, tok_out, tok_over, tok_go) = scratch
     a1, q, a2, s_ = (a1_0, a1_1, a1_2), (q_0, q_1, q_2), (a2_0, a2_1, a2_2), (s_0, s_1, s_2)
     size = m.shape[1]
     half, quarter = size // 2, size // 8
@@ -65,20 +66,22 @@
 
     pl.semaphore_wait(barrier, jnp.where(edge, len(mates) + 2, len(mates)))
 
-    def slot_of(o):
-        return jnp.where(low, o, 2 - o)
+    give = jnp.logical_or(z == mid, z == mid - 1)
+    slot_a = jnp.where(jnp.logical_xor(z == mid, first_one), piv[1, 0], piv[0, 0]) >> 4
+    for u in (0, 1, 2):
+        turned = slot_a + u
+        mp[u] = m[jnp.where(give, jnp.where(turned > 2, turned - 3, turned), jnp.where(low, u, 2 - u))]
 
     a1_sends = []
 
     def start_a1(o):
-        slot = slot_of(o)
         own = pltpu.make_async_copy(
-            m.at[slot, rows(k * half + f * quarter, quarter, quarter), :],
+            mp.at[o, rows(k * half + f * quarter, quarter, quarter), :],
             a1[o].at[f * 2 + k], a1_recv.at[o, f * 2 + k],
         )
         own.start()
         copy = rc(
-            m.at[slot, rows((1 - k) * half + g * quarter, quarter, quarter), :],
+            mp.at[o, rows((1 - k) * half + g * quarter, quarter, quarter), :],
             a1[o].at[g * 2 + k], a1_send.at[o, 0], a1_recv.at[o, g * 2 + k], partner,
         )
         copy.start()
@@ -89,7 +92,7 @@
                 ((x2, x, x2 * 8 + y * 2), (y2, y, x * 8 + y2 * 2 + 1))
             ):
                 copy = rc(
-                    m.at[slot, rows(n * half + pos * quarter, quarter, quarter), :],
+                    mp.at[o, rows(n * half + pos * quarter, quarter, quarter), :],
                     a1[o].at[here * 2 + k], a1_send.at[o, 2 * t + n - 1],
                     a1_recv.at[o, here * 2 + k], {"pcol": target},
                 )
@@ -137,7 +140,7 @@
     def dst(u, where):
         if u == 3:
             return xn.at[:, where, :]
-        return pn.at[:, slot_of(u), where, :]
+        return pn.at[:, u, where, :]
 
     def piece(u):
         return (w, s_[1], s_[2], lp)[u]
@@ -147,16 +150,17 @@
 
     g_sends = []
 
-    def start_g1(u):
+    def start_g1(u, note=True):
         pltpu.make_async_copy(piece(u), dst(u, spot(f, g)), g1_loc.at[u]).start()
         for t in (2, 1, 3):
             copy = rc(
                 piece(u), dst(u, spot(f, g)), g1_send.at[u, t - 1], g1_recv.at[u, g], dev(f, (g + t) & 3)
             )
             copy.start()
-            g_sends.append(copy)
-
-    def start_g2(u):
+            if note:
+                g_sends.append(copy)
+
+    def start_g2(u, note=True):
         pltpu.make_async_copy(piece(u), dst(u, spot(f, g)), g1_loc.at[u]).wait()
         for t in (1, 3, 2):
             j = (g + t) & 3
@@ -165,7 +169,8 @@
         for t in (2, 1, 3):
             copy = rc(block, block, g2_send.at[u, t - 1], g2_recv.at[u, f], dev((f + t) & 3, g))
             copy.start()
-            g_sends.append(copy)
+            if note:
+                g_sends.append(copy)
 
     def start_d(u):
         for t in (1, 3, 2):
@@ -230,7 +235,7 @@
 
         @pl.when(z == at)
         def _():
-            copy = pltpu.make_async_copy(m.at[0 if b == 0 else 2], rr.at[b], r_loc)
+            copy = pltpu.make_async_copy(mp.at[0], rr.at[b], r_loc)
             copy.start()
             copy.wait()
 
@@ -239,45 +244,47 @@
                     copy.start()
                 return carry
 
-            lax.fori_loop(0, n_chunk, send, 0)
-
-    give = jnp.logical_or(z == mid, z == mid - 1)
-    slot_a = jnp.where(jnp.logical_xor(z == mid, first_one), piv[1, 0], piv[0, 0]) >> 4
-
-    @pl.when(z == 0)
-    def _():
-        pl.semaphore_signal(tok_up, inc=1, device_id={"prow": z + 1}, device_id_type=MESH)
-
-    @pl.when(z == last)
-    def _():
-        pl.semaphore_signal(tok_down, inc=1, device_id={"prow": z - 1}, device_id_type=MESH)
-
-    @pl.when(jnp.logical_and(z >= 1, z <= mid))
-    def _():
-        pl.semaphore_wait(tok_up, 1)
-
-    @pl.when(jnp.logical_and(z >= 1, z < mid))
-    def _():
-        pl.semaphore_signal(tok_up, inc=1, device_id={"prow": z + 1}, device_id_type=MESH)
-
-    @pl.when(jnp.logical_and(z >= mid - 1, z < last))
-    def _():
-        pl.semaphore_wait(tok_down, 1)
-
-    @pl.when(jnp.logical_and(z >= mid, z < last))
-    def _():
-        pl.semaphore_signal(tok_down, inc=1, device_id={"prow": z - 1}, device_id_type=MESH)
+            lax.fori_loop(0, FIRST, send, 0)
 
     receiver = {"prow": jnp.where(z == mid, 0, last)}
-    sw_copy = rc(swsrc, sw, sw_send, sw_recv, receiver)
-    w_copy = rc(wsrc, w, w_send, w_recv, receiver)
+    sw_copy = rc(mp.at[0], sw, sw_send, sw_recv, receiver)
+    w_copy = rc(s_[0], w, w_send, w_recv, receiver)
+
+    def pass_in():
+        @pl.when(jnp.logical_and(h >= 1, h < mid - 1))
+        def _():
+            pl.semaphore_wait(tok_in, 1)
+
+        @pl.when(h >= 1)
+        def _():
+            pl.semaphore_signal(tok_in, inc=1, device_id=at_height(h - 1), device_id_type=MESH)
+
+    def pass_out():
+        @pl.when(h >= 1)
+        def _():
+            pl.semaphore_wait(tok_out, 1)
+
+        @pl.when(h < mid - 1)
+        def _():
+            pl.semaphore_signal(tok_out, inc=1, device_id=at_height(h + 1), device_id_type=MESH)
+
+    @pl.when(h < hub)
+    def _():
+        pass_out()
+        pass_in()
+
+    @pl.when(h >= hub)
+    def _():
+        pass_in()
+        pass_out()
 
     @pl.when(give)
     def _():
-        swsrc[...] = m[slot_a]
+        pl.semaphore_signal(tok_go, inc=1, device_id=other_edge, device_id_type=MESH)
+        pl.semaphore_wait(tok_go, 1)
         sw_copy.start()
 
-    begin = 90 + 33 * jnp.abs(h - hub)
+    begin = 130 + 33 * jnp.abs(h - hub)
 
     def mark(us):
         return jnp.where(relays, jnp.clip(jnp.maximum(us * 10 - begin, 0) // 12, 0, n_chunk), 0)
@@ -290,16 +297,9 @@
         done.append(marks[n])
 
     relay_to(0)
+
     finish_a1(0)
     start_a2(0)
-
-    @pl.when(jnp.logical_and(h >= 1, h < mid - 1))
-    def _():
-        pl.semaphore_wait(tok_in, 1)
-
-    @pl.when(h >= 1)
-    def _():
-        pl.semaphore_signal(tok_in, inc=1, device_id=at_height(h - 1), device_id_type=MESH)
 
     relay_to(1)
     finish_a1(1)
@@ -314,12 +314,28 @@
         pl.semaphore_signal(tok_over, inc=1, device_id=other_edge, device_id_type=MESH)
         pl.semaphore_wait(tok_over, 1)
 
+    @pl.when(give)
+    def _():
+        w_copy.start()
+
     for b, at in ((0, 0), (1, last)):
 
         @pl.when(z == at)
         def _():
             for t in (8, 7, 9, 6, 10, 5, 11, 4, 12, 3, 13, 2, 14, 1, 15):
                 corner(b, t).start()
+
+            def send(i, carry):
+                for copy in source_copies(b, i):
+                    copy.start()
+                return carry
+
+            lax.fori_loop(FIRST, n_chunk, send, 0)
+
+    @pl.when(jnp.logical_not(edge))
+    def _():
+        w[...] = s_[0][...]
+        start_g1(0, False)
 
     relay_to(2)
     finish_a1(2)
@@ -329,15 +345,12 @@
     relay_to(3)
     finish_a2(2)
 
-    @pl.when(give)
-    def _():
-        order_a = jnp.where(z == mid, 2 - slot_a, slot_a)
-        value = jnp.where(order_a == 1, s_[1][...], s_[0][...])
-        wsrc[...] = jnp.where(order_a == 2, s_[2][...], value)
-        w_copy.start()
-
     start_g1(2)
     relay_to(4)
+    @pl.when(jnp.logical_not(edge))
+    def _():
+        start_g2(0, False)
+
     start_g2(1)
     relay_to(5)
     for b, at in ((0, 0), (1, last)):
@@ -355,16 +368,16 @@
     @pl.when(edge)
     def _():
         w_copy.wait_recv()
-
-    @pl.when(jnp.logical_not(edge))
-    def _():
-        w[...] = s_[0][...]
-
-    start_g1(0)
+        start_g1(0, False)
+
     start_g2(3)
     relay_to(8)
     start_d(2)
-    start_g2(0)
+
+    @pl.when(edge)
+    def _():
+        start_g2(0, False)
+
     relay_to(9)
     start_d(3)
     chain(done[-1], jnp.where(relays, n_chunk, 0))
@@ -394,6 +407,10 @@
 
     for copy in a1_sends + a2_sends + g_sends:
         copy.wait_send()
+    for t in (1, 2, 3):
+        rc(w, w, g1_send.at[0, t - 1], g1_recv.at[0, g], partner).wait_send()
+        block = dst(0, rows(base, quarter, quarter))
+        rc(block, block, g2_send.at[0, t - 1], g2_recv.at[0, f], partner).wait_send()
 
     for b, at in ((0, 0), (1, last)):
 
@@ -435,8 +452,8 @@
         [vm((8, quarter, width), BF)] * 3
         + [vm((2, quarter, width), BF)] * 3
         + [vm((4, 2, PIECE, width), BF)] * 3
-        + [vm((2, PIECE, width), BF)] * 6
-        + [vm((size, width), BF)]
+        + [vm((2, PIECE, width), BF)] * 5
+        + [vm((slots, size, width), BF)]
         + [dma((3, 8)), dma((3, 8)), dma((3, 3)), dma((3, 4)), dma((4, 3)), dma((4, 4)), dma((4,))]
         + [dma((4, 3)), dma((4, 4)), dma((4,)), dma((4,))]
         + [dma((3, 2, n_chunk)), dma((2, n_chunk)), dma(())]
@@ -492,10 +509,14 @@
     def slot(s, carry):
         here = s * nrow + row
         held = jnp.where(here == b1, a1, jnp.where(here == b2, a2, here))
+        turned = s - jnp.where(row == nrow // 2, jnp.where(b1 == 0, a1, a2), jnp.where(b1 == 0, a2, a1)) // nrow
+        turned = jnp.where(turned < 0, turned + slots, turned)
+        give = jnp.logical_or(row == nrow // 2, row == nrow // 2 - 1)
+        unit = jnp.where(give, turned, jnp.where(row < nrow // 2, s, slots - 1 - s))
         old = jnp.where(here == held, blocks[s], swapped[...]).astype(F32) * keep(held, col)
-        left1 = (dot(panels[0, s], inv[0]) * keep(held, c1)).astype(BF)
+        left1 = (dot(panels[0, unit], inv[0]) * keep(held, c1)).astype(BF)
         step1 = (old - dot(left1, tops[one]) * own1).astype(BF)
-        column2 = panels[1, s].astype(F32) * keep(held, c2) - dot(left1, corners[one]) * cross12
+        column2 = panels[1, unit].astype(F32) * keep(held, c2) - dot(left1, corners[one]) * cross12
         left2 = dot(column2.astype(BF), inv[1]).astype(BF)
         out[s] = (step1.astype(F32) - dot(left2, upper[...])).astype(BF)
 

time: 91 us -> 84.8 us (0.932)
  the two profiles are of different devices: /device:TPU:34 before, /device:TPU:32 now
where the time goes in v3:
time: 84.8 us; the launch traced here: 84.6 us
  Pallas kernels  83.2 us (98%)
  local copies, waits for them, and re-layouts  1.41 us (2%)
    pallas_call x1, Pallas kernels, run_gather(): pl.pallas_call(gather, out_shape=[jax.ShapeDtypeStruct((2, slots, size, w...  73.1 us
    pallas_call x1, Pallas kernels, run_update(): pl.pallas_call(update, out_shape=jax.ShapeDtypeStruct(blocks.shape, BF),...  10.1 us

profile of v3, /device:TPU:32, one launch (start us, length us, event | category | flops | bytes accessed | tf_op | source)
XLA Modules:
  0.0 84.6 jit_solution(3628045276970577565)
XLA Ops:
  0.0 1.4 %copy.5.pat = s32[48,32]{1,0:T(8,128)} copy(s32[48,32]{0,1:T(8,128)} %param.5) | data formatting | bytes 12288 | tf_op args[1]
  1.4 73.1 %gather.1 = (bf16[2,3,512,512]{3,2,1,0:T(8,128)(2,1)}, bf16[2,512,512]{2,1,0:T(8,128)(2,1)}, bf16[2,512,512]{2,1,0:T(8,128)(2,1)}, bf16[512,512]{1,0:T(8,128)(2,1)}) custom-call(s32[2,3]{1,0:T(2,128)} %piv.3, bf16[3,512,512]{2,1,0:T(8,128)(2,1)} %bitcast.4), custom_call_target="tpu_custom_call" | custom-call | tf_op jit(solution)/shard_map/gather/pallas_call | solution.py:464
  74.5 10.1 %update.1 = bf16[3,512,512]{2,1,0:T(8,128)(2,1)} custom-call(s32[2,3]{1,0:T(2,128)} %piv.3, s32[48,32]{1,0:T(8,128)} %copy.5.pat, bf16[3,512,512]{2,1,0:T(8,128)(2,1)} %bitcast.5, bf16[2,3,512,512]{3,2,1,0:T(8,128)(2,1)} %get-tuple-element.9.panels, bf16[2,512,512]{2,1,0:T(8,128)(2,1)} %get-tuple-element.10.corners, ...), custom_call_target="tpu_custom_call" | custom-call | tf_op jit(solution)/shard_map/update/pallas_call | solution.py:547

commit v4 on v3

--- a/solution.py
+++ b/solution.py
@@ -17,7 +17,7 @@
     (a1_0, a1_1, a1_2, q_0, q_1, q_2, a2_0, a2_1, a2_2, s_0, s_1, s_2, lp, w, mp,
      a1_send, a1_recv, a2_send, a2_recv, g1_send, g1_recv, g1_loc, g2_send, g2_recv,
      d_send, d_recv, r_send, r_recv, r_loc, l_send, l_recv,
-     sw_send, sw_recv, w_send, w_recv, tok_in, tok_out, tok_over, tok_go) = scratch
+     sw_send, sw_recv, w_send, w_recv, tok_in, tok_over) = scratch
     a1, q, a2, s_ = (a1_0, a1_1, a1_2), (q_0, q_1, q_2), (a2_0, a2_1, a2_2), (s_0, s_1, s_2)
     size = m.shape[1]
     half, quarter = size // 2, size // 8
@@ -57,16 +57,22 @@
     mates.append({"prow": (z + last) & last})
     for mate in mates:
         pl.semaphore_signal(barrier, inc=1, device_id=mate, device_id_type=MESH)
-    hub = mid // 2
+    hub = mid // 2 - 1
 
     @pl.when(jnp.logical_or(z == hub, z == last - hub))
     def _():
         for at in (0, last):
             pl.semaphore_signal(barrier, inc=1, device_id={"prow": at}, device_id_type=MESH)
 
-    pl.semaphore_wait(barrier, jnp.where(edge, len(mates) + 2, len(mates)))
-
     give = jnp.logical_or(z == mid, z == mid - 1)
+
+    @pl.when(edge)
+    def _():
+        pl.semaphore_signal(barrier, inc=1, device_id={"prow": z ^ mid}, device_id_type=MESH)
+
+    extra = jnp.where(edge, 2, jnp.where(give, 1, 0))
+    pl.semaphore_wait(barrier, len(mates) + extra)
+
     slot_a = jnp.where(jnp.logical_xor(z == mid, first_one), piv[1, 0], piv[0, 0]) >> 4
     for u in (0, 1, 2):
         turned = slot_a + u
@@ -230,6 +236,13 @@
 
     for o in (0, 1, 2):
         start_a1(o)
+    receiver = {"prow": jnp.where(z == mid, 0, last)}
+    sw_copy = rc(mp.at[0], sw, sw_send, sw_recv, receiver)
+
+    @pl.when(give)
+    def _():
+        sw_copy.start()
+
 
     for b, at in ((0, 0), (1, last)):
 
@@ -246,8 +259,6 @@
 
             lax.fori_loop(0, FIRST, send, 0)
 
-    receiver = {"prow": jnp.where(z == mid, 0, last)}
-    sw_copy = rc(mp.at[0], sw, sw_send, sw_recv, receiver)
     w_copy = rc(s_[0], w, w_send, w_recv, receiver)
 
     def pass_in():
@@ -259,30 +270,7 @@
         def _():
             pl.semaphore_signal(tok_in, inc=1, device_id=at_height(h - 1), device_id_type=MESH)
 
-    def pass_out():
-        @pl.when(h >= 1)
-        def _():
-            pl.semaphore_wait(tok_out, 1)
-
-        @pl.when(h < mid - 1)
-        def _():
-            pl.semaphore_signal(tok_out, inc=1, device_id=at_height(h + 1), device_id_type=MESH)
-
-    @pl.when(h < hub)
-    def _():
-        pass_out()
-        pass_in()
-
-    @pl.when(h >= hub)
-    def _():
-        pass_in()
-        pass_out()
-
-    @pl.when(give)
-    def _():
-        pl.semaphore_signal(tok_go, inc=1, device_id=other_edge, device_id_type=MESH)
-        pl.semaphore_wait(tok_go, 1)
-        sw_copy.start()
+    pass_in()
 
     begin = 130 + 33 * jnp.abs(h - hub)
 
@@ -459,7 +447,7 @@
         + [dma((3, 2, n_chunk)), dma((2, n_chunk)), dma(())]
         + [dma((15,)), dma((2,))]
         + [dma(())] * 4
-        + [pltpu.SemaphoreType.REGULAR] * 4
+        + [pltpu.SemaphoreType.REGULAR] * 2
     )
     return pl.pallas_call(
         gather,
@@ -470,7 +458,7 @@
             jax.ShapeDtypeStruct((size, width), BF),
         ],
         in_specs=[pl.BlockSpec(memory_space=pltpu.SMEM), pl.BlockSpec(memory_space=pltpu.VMEM)],
-        out_specs=[pl.BlockSpec(memory_space=pltpu.VMEM)] * 4,
+        out_specs=[pl.BlockSpec(memory_space=pl.ANY)] * 4,
         scratch_shapes=scratch,
         compiler_params=pltpu.CompilerParams(collective_id=0, has_side_effects=True),
         name="gather",
@@ -488,7 +476,7 @@
     two = 1 - one
 
     def keep(i, j):
-        return pat[i, j].astype(F32)
+        return pat[j, i].astype(F32)
 
     def dot(left, right):
         return jnp.dot(left, right, preferred_element_type=F32)
@@ -558,7 +546,7 @@
     slots, size, _, width = matrix.shape
     blocks = matrix.reshape(slots, size, width)
     moved = run_gather(pivots, blocks)
-    return run_update(pivots, pattern, blocks, *moved, inverses).reshape(matrix.shape)
+    return run_update(pivots, pattern.T, blocks, *moved, inverses).reshape(matrix.shape)
 
 
 def solution(mesh):

time: 84.8 us -> 76.1 us (0.90)
  the two profiles are of different devices: /device:TPU:32 before, /device:TPU:193 now
where the time goes in v4:
time: 76.1 us; the launch traced here: 76 us
  Pallas kernels  76 us (100%)
    pallas_call x1, Pallas kernels, run_gather(): pl.pallas_call(gather, out_shape=[jax.ShapeDtypeStruct((2, slots, size, w...  65.9 us
    pallas_call x1, Pallas kernels, run_update(): pl.pallas_call(update, out_shape=jax.ShapeDtypeStruct(blocks.shape, BF),...  10.1 us

profile of v4, /device:TPU:193, one launch (start us, length us, event | category | flops | bytes accessed | tf_op | source)
XLA Modules:
  0.0 76.0 jit_solution(5232963423826754410)
XLA Ops:
  0.0 65.9 %gather.1 = (bf16[2,3,512,512]{3,2,1,0:T(8,128)(2,1)}, bf16[2,512,512]{2,1,0:T(8,128)(2,1)}, bf16[2,512,512]{2,1,0:T(8,128)(2,1)}, bf16[512,512]{1,0:T(8,128)(2,1)}) custom-call(s32[2,3]{1,0:T(2,128)} %piv.3, bf16[3,512,512]{2,1,0:T(8,128)(2,1)} %bitcast.5), custom_call_target="tpu_custom_call" | custom-call | tf_op jit(solution)/shard_map/gather/pallas_call | solution.py:452
  65.9 10.1 %update.1 = bf16[3,512,512]{2,1,0:T(8,128)(2,1)} custom-call(s32[2,3]{1,0:T(2,128)} %piv.3, s32[32,48]{1,0:T(8,128)} %bitcast.7, bf16[3,512,512]{2,1,0:T(8,128)(2,1)} %bitcast.6, bf16[2,3,512,512]{3,2,1,0:T(8,128)(2,1)} %get-tuple-element.9.panels, bf16[2,512,512]{2,1,0:T(8,128)(2,1)} %get-tuple-element.10.corners, ...), custom_call_target="tpu_custom_call" | custom-call | tf_op jit(solution)/shard_map/update/pallas_call | solution.py:535

commit v5 on v4

--- a/solution.py
+++ b/solution.py
@@ -465,7 +465,14 @@
     )(pivots, blocks)
 
 
-def update(piv, pat, blocks, panels, corners, tops, swapped, inv, out, lead, upper):
+def update(piv, pat, blocks_far, panels_far, corners, tops, swapped_far, inv, out, lead, upper, blocks, panels, swapped, sems):
+    loads = [
+        pltpu.make_async_copy(panels_far, panels, sems.at[0]),
+        pltpu.make_async_copy(blocks_far, blocks, sems.at[1]),
+        pltpu.make_async_copy(swapped_far, swapped, sems.at[2]),
+    ]
+    for load in loads:
+        load.start()
     slots, size, width = blocks.shape
     row = lax.axis_index("prow")
     col = lax.axis_index("pcol")
@@ -493,6 +500,9 @@
     def _():
         old = tops[two].astype(F32) * keep(b2, col)
         upper[...] = (old - dot(lead[...], tops[one]) * own1).astype(BF)
+
+    for load in loads:
+        load.wait()
 
     def slot(s, carry):
         here = s * nrow + row
@@ -532,12 +542,15 @@
 def run_update(pivots, pattern, blocks, panels, corners, tops, swapped, inverses):
     slots, size, width = blocks.shape
     smem, vmem = pl.BlockSpec(memory_space=pltpu.SMEM), pl.BlockSpec(memory_space=pltpu.VMEM)
+    far = pl.BlockSpec(memory_space=pl.ANY)
     return pl.pallas_call(
         update,
         out_shape=jax.ShapeDtypeStruct(blocks.shape, BF),
-        in_specs=[smem, smem] + [vmem] * 6,
+        in_specs=[smem, smem, far, far, vmem, vmem, far, vmem],
         out_specs=vmem,
-        scratch_shapes=[pltpu.VMEM((size, width), BF)] * 2,
+        scratch_shapes=[pltpu.VMEM((size, width), BF)] * 2
+        + [pltpu.VMEM(blocks.shape, BF), pltpu.VMEM(panels.shape, BF), pltpu.VMEM((size, width), BF)]
+        + [pltpu.SemaphoreType.DMA((3,))],
         name="update",
     )(pivots, pattern, blocks, panels, corners, tops, swapped, inverses)
 

time: 76.1 us -> 76.3 us (level)
  no operation moved by 1% of the time
where the time goes in v5:
time: 76.3 us; the launch traced here: 76.1 us
  Pallas kernels  76.1 us (100%)
    pallas_call x1, Pallas kernels, run_gather(): pl.pallas_call(gather, out_shape=[jax.ShapeDtypeStruct((2, slots, size, w...  65.9 us
    pallas_call x1, Pallas kernels, run_update(): pl.pallas_call(update, out_shape=jax.ShapeDtypeStruct(blocks.shape, BF),...  10.2 us

profile of v5, /device:TPU:193, one launch (start us, length us, event | category | flops | bytes accessed | tf_op | source)
XLA Modules:
  0.0 76.1 jit_solution(12346691516318003745)
XLA Ops:
  0.0 65.9 %gather.1 = (bf16[2,3,512,512]{3,2,1,0:T(8,128)(2,1)}, bf16[2,512,512]{2,1,0:T(8,128)(2,1)}, bf16[2,512,512]{2,1,0:T(8,128)(2,1)}, bf16[512,512]{1,0:T(8,128)(2,1)}) custom-call(s32[2,3]{1,0:T(2,128)} %piv.3, bf16[3,512,512]{2,1,0:T(8,128)(2,1)} %bitcast.5), custom_call_target="tpu_custom_call" | custom-call | tf_op jit(solution)/shard_map/gather/pallas_call | solution.py:452
  65.9 10.2 %update.1 = bf16[3,512,512]{2,1,0:T(8,128)(2,1)} custom-call(s32[2,3]{1,0:T(2,128)} %piv.3, s32[32,48]{1,0:T(8,128)} %bitcast.7, bf16[3,512,512]{2,1,0:T(8,128)(2,1)} %bitcast.6, bf16[2,3,512,512]{3,2,1,0:T(8,128)(2,1)} %get-tuple-element.9.panels_far, bf16[2,512,512]{2,1,0:T(8,128)(2,1)} %get-tuple-element.10.corners, ...), custom_call_target="tpu_custom_call" | custom-call | tf_op jit(solution)/shard_map/update/pallas_call | solution.py:546
